TPU v7x, 32 devices: a whole 2x2x4 slice. The times are simulated.
32 devices in a mesh: clip: 2 (over x), seq: 16 (over z, y, core).
Axes of the slice: x: 2, y: 2, z: 4, core: 2. Of those that a mesh axis runs over, the one named last changes fastest.
Arguments:
- hidden: bfloat16 [2, 1792, 1536], P(None, ('clip', 'seq')), parts along dimension 1, may hold values from -6 to 6
- latent: float32 [1792, 100], P(('clip', 'seq')), parts along dimension 0, may hold values from -6 to 6
- lengths: int32 [2], P('clip'), parts along dimension 0, may hold values from 448 to 896
- step_index: int32 [1], replicated, may hold values from 0 to 31
- guidance: float32 [1], replicated, may hold values from 1.5 to 2.5
- modulation: float32 [5, 1536], replicated, may hold values from -2.5 to 2.5
- conv_kernel: float32 [31, 1536], replicated, may hold values from -1 to 1
- w_qkv: bfloat16 [1536, 3072], replicated, may hold values from -1 to 1
- w_out: bfloat16 [1024, 1536], replicated, may hold values from -0.1875 to 0.1875
- w_mel: bfloat16 [1536, 100], replicated, may hold values from -0.15625 to 0.15625
Outputs:
- velocity: float32 [1792, 100], P(('clip', 'seq')), parts along dimension 0
- estimate: float32 [1792, 100], P(('clip', 'seq')), parts along dimension 0
There are 2 independent parts, one for each index of `clip`. A program takes and returns all parts, laid end to end along the dimension named above; an argument that names none is the same for every part. Nothing has to cross between parts.
All inputs are finite; a program needn't handle non-finite values.
Results may differ from a plain program's by a relative error of at most 0.0061.
Values may be sent and summed in bfloat16 or wider, within the bound.
No kernel may reach another device: no remote copies, remote signals or barrier semaphores. Data moves between devices by JAX's collectives and lax.ppermute only.
A program may use at most 192 MiB of HBM per device.

v0:
```python
import jax
import jax.numpy as jnp
from jax import lax
from jax.sharding import PartitionSpec as P

HEADS = 16
HEAD_DIM = 64
KERNEL = 31
STEPS = 32
EPSILON = 1e-06
NEGATIVE = -1e30


def extended(cells, sides, width):
    for axis, dim in sides:
        count = lax.axis_size(axis)
        ends = count - 1
        head = lax.slice_in_dim(cells, 0, width, axis=dim)
        tail = lax.slice_in_dim(cells, cells.shape[dim] - width, cells.shape[dim], axis=dim)
        cells = jnp.concatenate(
            [
                lax.ppermute(tail, axis, [(i, (i + 1) % count) for i in range(ends)]),
                cells,
                lax.ppermute(head, axis, [((i + 1) % count, i) for i in range(ends)]),
            ],
            axis=dim,
        )
    return cells


def from_partner(shard, axis, apart):
    return lax.ppermute(shard, axis, [(i, i ^ 1 << apart) for i in range(lax.axis_size(axis))])


def layer_norm(values, shift_row, scale_row):
    mean_value = jnp.mean(values, axis=-1, keepdims=True)
    centered = values - mean_value
    variance = jnp.mean(centered * centered, axis=-1, keepdims=True)
    return centered * lax.rsqrt(variance + EPSILON) * (1.0 + scale_row) + shift_row


def mish(values):
    return values * jnp.tanh(jax.nn.softplus(values))


def rotate(values, positions):
    half_dim = values.shape[-1] // 2
    inverse = 10000.0 ** (-jnp.arange(half_dim, dtype=jnp.float32) / half_dim)
    angles = positions.astype(jnp.float32)[:, None] * inverse[None, :]
    cosine = jnp.cos(angles)[:, None, :]
    sine_table = jnp.sin(angles)[:, None, :]
    lower_half = values[..., :half_dim]
    upper_half = values[..., half_dim:]
    return jnp.concatenate(
        [
            lower_half * cosine - upper_half * sine_table,
            upper_half * cosine + lower_half * sine_table,
        ],
        axis=-1,
    )


def to_groups(values, subs):
    copies, frame_rows, _ = values.shape
    grouped = values.reshape(copies, subs, frame_rows // subs, HEADS, HEAD_DIM).transpose(
        0, 3, 1, 2, 4
    )
    return grouped.reshape(copies * HEADS * subs, frame_rows // (2 * subs), 2 * HEAD_DIM)


def from_groups(grouped, copies, frame_rows, subs):
    split = grouped.reshape(copies, HEADS, subs, frame_rows // subs, HEAD_DIM).transpose(
        0, 2, 3, 1, 4
    )
    return split.reshape(copies, frame_rows, HEADS * HEAD_DIM)


def block_size_for(row_total):
    for candidate in range(1024, 7, -8):
        if row_total % candidate == 0:
            return candidate
    return row_total


def attend_local(query_flat, key_flat, value_flat, key_live):
    groups, query_total, _ = query_flat.shape
    block_rows = block_size_for(query_total)
    blocks = query_flat.reshape(groups, query_total // block_rows, block_rows, HEAD_DIM).transpose(
        1, 0, 2, 3
    )
    scale_factor = HEAD_DIM ** (-0.5)
    live_mask = key_live[None, None, :]

    def one_block(block):
        scores = (
            jnp.einsum("gqd,gkd->gqk", block, key_flat, preferred_element_type=jnp.float32)
            * scale_factor
        )
        scores = jnp.where(live_mask, scores, NEGATIVE)
        row_peak = jnp.max(scores, axis=-1, keepdims=True)
        weights = jnp.where(live_mask, jnp.exp(scores - row_peak), 0.0)
        weight_sum = jnp.sum(weights, axis=-1)
        weighted = jnp.einsum(
            "gqk,gkd->gqd",
            weights.astype(jnp.bfloat16),
            value_flat,
            preferred_element_type=jnp.float32,
        )
        return (weighted / weight_sum[..., None]).astype(jnp.bfloat16)

    results = lax.map(one_block, blocks)
    return results.transpose(1, 0, 2, 3).reshape(groups, query_total, HEAD_DIM)


def per_device(
    hidden, latent, lengths, step_index, guidance, modulation, conv_kernel, w_qkv, w_out, w_mel
):
    copies, frame_rows, model_width = hidden.shape
    offset = lax.axis_index("seq") * frame_rows
    positions = offset + jnp.arange(frame_rows, dtype=jnp.int32)
    length = lengths[0]
    is_live = positions < length
    masked = hidden * is_live[None, :, None].astype(jnp.bfloat16)
    half_width = KERNEL // 2
    padded = extended(masked, (("seq", 1),), half_width)
    convolved = jnp.zeros(hidden.shape, jnp.float32)
    for tap_index in range(KERNEL):
        convolved = convolved + conv_kernel[tap_index] * padded[
            :, tap_index : tap_index + frame_rows, :
        ].astype(jnp.float32)
    residual = hidden.astype(jnp.float32) + mish(convolved)
    normed = layer_norm(residual, modulation[0], modulation[1]).astype(jnp.bfloat16)
    projected = jnp.dot(normed.reshape(-1, model_width), w_qkv, preferred_element_type=jnp.float32)
    projected = projected.reshape(copies, frame_rows, 3, HEADS, HEAD_DIM)
    queries = rotate(projected[:, :, 0], positions).astype(jnp.bfloat16)
    keys_all = (
        rotate(projected[:, :, 1], positions)
        .astype(jnp.bfloat16)
        .reshape(copies, frame_rows, HEADS * HEAD_DIM)
    )
    values_all = (
        projected[:, :, 2].astype(jnp.bfloat16).reshape(copies, frame_rows, HEADS * HEAD_DIM)
    )
    seq_size = lax.axis_size("seq")
    subs = max(1, seq_size // (2 * HEADS))
    sub_index = lax.axis_index("seq") % subs
    part_rows = frame_rows // subs
    queries_flat = queries.reshape(copies, frame_rows, HEADS * HEAD_DIM)
    sent = (to_groups(queries_flat, subs), to_groups(keys_all, subs), to_groups(values_all, subs))
    query_group, key_group, value_group = (
        lax.all_to_all(sent[0], "seq", split_axis=0, concat_axis=1, tiled=True),
        lax.all_to_all(sent[1], "seq", split_axis=0, concat_axis=1, tiled=True),
        lax.all_to_all(sent[2], "seq", split_axis=0, concat_axis=1, tiled=True),
    )

    def key_positions(sub_id):
        source_start = jnp.arange(seq_size, dtype=jnp.int32)[:, None] * frame_rows
        return (
            source_start + sub_id * part_rows + jnp.arange(part_rows, dtype=jnp.int32)[None, :]
        ).reshape(-1)

    key_rows = key_positions(sub_index)
    if subs > 1:
        other_keys, other_values = from_partner((key_group, value_group), "seq", 0)
        key_group = jnp.concatenate([key_group, other_keys], axis=1)
        value_group = jnp.concatenate([value_group, other_values], axis=1)
        key_rows = jnp.concatenate([key_rows, key_positions(1 - sub_index)])
    groups = query_group.shape[0]
    query_flat = query_group.reshape(groups, -1, HEAD_DIM)
    key_flat = key_group.reshape(groups, -1, HEAD_DIM)
    value_flat = value_group.reshape(groups, -1, HEAD_DIM)
    attended_group = attend_local(query_flat, key_flat, value_flat, key_rows < length)
    returned = lax.all_to_all(
        attended_group.reshape(groups, -1, 2 * HEAD_DIM),
        "seq",
        split_axis=1,
        concat_axis=0,
        tiled=True,
    )
    attended = from_groups(returned, copies, frame_rows, subs)
    branch = jnp.dot(
        attended.reshape(copies * frame_rows, -1), w_out, preferred_element_type=jnp.float32
    )
    after = residual + modulation[2] * branch.reshape(copies, frame_rows, model_width)
    final_norm = layer_norm(after, modulation[3], modulation[4]).astype(jnp.bfloat16)
    speed = jnp.dot(final_norm.reshape(-1, model_width), w_mel, preferred_element_type=jnp.float32)
    speed = speed.reshape(copies, frame_rows, -1)
    guided = speed[0] + guidance[0] * (speed[0] - speed[1])
    velocity = jnp.where(is_live[:, None], guided, 0.0)
    progress = step_index[0].astype(jnp.float32) / STEPS
    time_now = 1.0 - jnp.cos(0.5 * jnp.pi * progress)
    estimate = latent + (1.0 - time_now) * velocity
    return (velocity, estimate)


def solution(mesh):
    return jax.shard_map(
        per_device,
        mesh=mesh,
        in_specs=(
            P(None, ("clip", "seq"), None),
            P(("clip", "seq"), None),
            P("clip"),
            P(),
            P(),
            P(),
            P(),
            P(),
            P(),
            P(),
        ),
        out_specs=(P(("clip", "seq"), None), P(("clip", "seq"), None)),
        check_vma=False,
    )
```

profile of v0, /device:TPU:0, one launch (start us, length us, event | category | flops | bytes accessed | tf_op | source)
XLA Modules:
  0.0 131.8 jit_solution(2257580926688157541)
XLA Ops:
  1.5 1.2 broadcast_multiply_fusion
  3.4 3.0 %collective-permute-start = (bf16[2,15,1536]{2,1,0:T(8,128)(2,1)}, bf16[2,15,1536]{2,1,0:T(8,128)(2,1)}, u32[]{:S(2)}, u32[]{:S(2)}) collective-permute-start(bf16[2,15,1536]{2,1,0:T(8,128)(2,1)} %get-tuple-element.74), channel_id=1, source_target_pairs={{0,1},{1,2},{2,3},{3,4},{4,5},{5,6},{6,7},{7,8},{8,9},{9,10},{10,1... | collective-permute-start | bytes 276488 | tf_op jit(solution)/shard_map/ppermute | solution.py:22
  6.4 1.3 collective-permute-start.1
  7.7 2.5 %slice_reduce_fusion.33 = (f32[1536]{0:T(1024)S(1)}, f32[1536]{0:T(1024)S(1)}, f32[1536]{0:T(1024)S(1)}, f32[1536]{0:T(1024)S(1)}, f32[1536]{0:T(1024)S(1)}, /*i...) fusion(f32[31,1536]{1,0:T(8,128)} %param.16), kind=kLoop, calls=%fused_computation.177 | loop fusion | bytes 233472 | tf_op jit(solution)/shard_map/slice | solution.py:128
  10.2 2.1 %slice_reduce_fusion.32 = (f32[1536]{0:T(1024)}, f32[1536]{0:T(1024)}, f32[1536]{0:T(1024)}, f32[1536]{0:T(1024)}, f32[1536]{0:T(1024)}, /*index=5*/f32[1536]{0:...) fusion(f32[31,1536]{1,0:T(8,128)} %param.16), kind=kLoop, calls=%fused_computation.176 | loop fusion | bytes 147456 | tf_op jit(solution)/shard_map/slice | solution.py:128
  12.3 12.7 %copy.34 = bf16[1536,3072]{0,1:T(8,128)(2,1)} copy(bf16[1536,3072]{1,0:T(8,128)(2,1)} %param.17) | data formatting | bytes 18874368 | tf_op args[7]
  25.2 1.7 %add_reduce_fusion = (f32[1536]{0:T(1024)S(1)}, f32[1536]{0:T(1024)S(1)}, f32[1536]{0:T(1024)S(1)}, f32[1536]{0:T(1024)}, f32[1536]{0:T(1024)}) fusion(f32[5,1536]{1,0:T(8,128)} %param.15), kind=kLoop, calls=%fused_computation.143 | loop fusion | flops 3072 | bytes 61440 | tf_op jit(solution)/shard_map/add | solution.py:39
  26.9 8.2 %fusion.74 = (f32[2,56]{1,0:T(2,128)S(1)}, f32[2,56,1536]{2,1,0:T(8,128)S(1)}) fusion(bf16[2,15,1536]{2,1,0:T(8,128)(2,1)} %collective-permute-done.1, bf16[2,56,1536]{2,1,0:T(8,128)(2,1)S(1)} %broadcast_multiply_fusion, f32[1536]{0:T(1024)} %get-tuple-element.55, f32[1536]{0:T(1024)} %get-tuple-element.56, f32[1536]{0:T(1024)S(1)} %get-tuple-element.27, ...), kind=kLoop, calls=%fused_computation.189 | loop fusion | flops 33030032 | bytes 1751488 | tf_op jit(solution)/shard_map/reduce_sum | solution.py:36
  35.4 7.3 %fusion.60 = f32[2,56,3,16,64]{4,1,3,2,0:T(8,128)S(1)} fusion(bf16[3,16,64,1536,1]{3,2,1,0,4:T(8,128)(2,1)} %bitcast.90, f32[2,56,1536]{2,1,0:T(8,128)S(1)} %get-tuple-element.65, f32[1536]{0:T(1024)S(1)} %get-tuple-element.58, f32[1536]{0:T(1024)S(1)} %get-tuple-element.59, f32[2,56]{1,0:T(2,128)S(1)} %add_rsqrt_fusion.1, ...), kind=kOutput, calls=%fused_computation.123 | convolution fusion | flops 1057824768 | bytes 11514752 | tf_op jit(solution)/shard_map/dot_general | solution.py:133
  42.9 1.7 %fusion.28 = (bf16[2,1,56,16,32]{4,2,3,0,1:T(8,128)(2,1)S(1)}, bf16[2,1,56,16,32]{4,2,3,0,1:T(8,128)(2,1)S(1)}, bf16[2,1,56,16,32]{4,2,3,0,1:T(8,128)(2,1)}, bf16[2,1,56,16,32]{4,2,3,0,1:T(8,128)(2,1)}) fusion(f32[2,56,16,64]{3,1,2,0:T(8,128)S(1)} %get-tuple-element.68, f32[56,32]{1,0:T(8,128)S(1)} %get-tuple-element.79, f32[56,32]{1,0:T(8,128)S(1)} %get-tuple-element.78, ...), kind=kLoop, calls=%fused_computation.61 | loop fusion | flops 917504 | bytes 1390592 | tf_op jit(solution)/shard_map/concatenate | solution.py:54
  44.5 1.0 maximum_bitcast_fusion.1
  45.6 2.0 %reshape.294 = bf16[32,28,128]{2,1,0:T(8,128)(2,1)} reshape(bf16[2,16,1,56,64]{4,3,1,0,2:T(8,128)(2,1)} %maximum_bitcast_fusion.1) | data formatting | bytes 458752 | tf_op jit(solution)/shard_map/reshape | solution.py:68
  47.5 8.7 %all-to-all-start.1 = ((bf16[32,28,128]{2,1,0:T(8,128)(2,1)}), bf16[32,28,128]{2,1,0:T(8,128)(2,1)S(1)}, u32[]{:S(2)}, u32[]{:S(2)}) async-start(bf16[32,28,128]{2,1,0:T(8,128)(2,1)} %reshape.294), calls=%async_computation.1 | async-start | bytes 524288 | tf_op jit(solution)/shard_map/all_to_all | solution.py:152
  56.2 2.2 %maximum_bitcast_fusion = bf16[2,16,1,56,64]{4,3,1,0,2:T(8,128)(2,1)} fusion(bf16[2,1,56,16,32]{4,2,3,0,1:T(8,128)(2,1)} %get-tuple-element.76, bf16[2,1,56,16,32]{4,2,3,0,1:T(8,128)(2,1)} %get-tuple-element.77), kind=kLoop, calls=%fused_computation.64 | loop fusion | flops 458752 | bytes 458752 | tf_op jit(solution)/shard_map/transpose | solution.py:65
  58.4 2.0 %reshape.293 = bf16[32,28,128]{2,1,0:T(8,128)(2,1)} reshape(bf16[2,16,1,56,64]{4,3,1,0,2:T(8,128)(2,1)} %maximum_bitcast_fusion) | data formatting | bytes 458752 | tf_op jit(solution)/shard_map/reshape | solution.py:68
  60.4 5.9 %all-to-all-done.1 = bf16[32,28,128]{2,1,0:T(8,128)(2,1)S(1)} async-done(((bf16[32,28,128]{2,1,0:T(8,128)(2,1)}), bf16[32,28,128]{2,1,0:T(8,128)(2,1)S(1)}, u32[]{:S(2)}, u32[]{:S(2)}) %all-to-all-start.1) | async-done | bytes 229408 | tf_op jit(solution)/shard_map/all_to_all | solution.py:152
  66.2 4.2 %all-to-all-start = ((bf16[32,28,128]{2,1,0:T(8,128)(2,1)}), bf16[32,28,128]{2,1,0:T(8,128)(2,1)}, u32[]{:S(2)}, u32[]{:S(2)}) async-start(bf16[32,28,128]{2,1,0:T(8,128)(2,1)} %reshape.293), calls=%async_computation | async-start | bytes 524288 | tf_op jit(solution)/shard_map/all_to_all | solution.py:151
  70.4 2.0 %fusion.30 = bf16[2,16,1,56,64]{4,3,1,0,2:T(8,128)(2,1)} fusion(f32[2,56,3,16,64]{4,1,3,2,0:T(8,128)} %copy-done.2), kind=kLoop, calls=%fused_computation.63 | loop fusion | bytes 458752 | tf_op jit(solution)/shard_map/transpose | solution.py:65
  72.5 2.0 %reshape.296 = bf16[32,28,128]{2,1,0:T(8,128)(2,1)} reshape(bf16[2,16,1,56,64]{4,3,1,0,2:T(8,128)(2,1)} %fusion.30) | data formatting | bytes 458752 | tf_op jit(solution)/shard_map/reshape | solution.py:68
  74.4 6.0 %all-to-all-done = bf16[32,28,128]{2,1,0:T(8,128)(2,1)} async-done(((bf16[32,28,128]{2,1,0:T(8,128)(2,1)}), bf16[32,28,128]{2,1,0:T(8,128)(2,1)}, u32[]{:S(2)}, u32[]{:S(2)}) %all-to-all-start) | async-done | bytes 229408 | tf_op jit(solution)/shard_map/all_to_all | solution.py:151
  80.4 4.4 %all-to-all-start.2 = ((bf16[32,28,128]{2,1,0:T(8,128)(2,1)}), bf16[32,28,128]{2,1,0:T(8,128)(2,1)}, u32[]{:S(2)}, u32[]{:S(2)}) async-start(bf16[32,28,128]{2,1,0:T(8,128)(2,1)} %reshape.296), calls=%async_computation.2 | async-start | bytes 524288 | tf_op jit(solution)/shard_map/all_to_all | solution.py:153
  85.7 2.0 %reshape.295 = bf16[2,896,64]{2,1,0:T(8,128)(2,1)} reshape(bf16[2,16,28,128]{3,2,1,0:T(8,128)(2,1)} %bitcast.94) | data formatting | bytes 458752 | tf_op jit(solution)/shard_map/reshape | solution.py:170
  88.7 1.0 squeeze.26
  89.7 4.9 %all-to-all-done.2 = bf16[32,28,128]{2,1,0:T(8,128)(2,1)} async-done(((bf16[32,28,128]{2,1,0:T(8,128)(2,1)}), bf16[32,28,128]{2,1,0:T(8,128)(2,1)}, u32[]{:S(2)}, u32[]{:S(2)}) %all-to-all-start.2) | async-done | bytes 229408 | tf_op jit(solution)/shard_map/all_to_all | solution.py:153
  96.6 5.7 %fusion.79 = (f32[2,896]{1,0:T(2,128)S(1)}, bf16[2,896,896]{1,2,0:T(8,128)(2,1)}) fusion(pred[896]{0:T(1024)(128)(4,1)S(1)} %lt.36, bf16[2,896,64]{2,1,0:T(8,128)(2,1)} %squeeze.26, bf16[2,896,64]{2,1,0:T(8,128)(2,1)} %reshape.295), kind=kOutput, calls=%fused_computation.192 | convolution fusion | flops 215155584 | bytes 3678080 | tf_op jit(solution)/shard_map/while/body/eval_jaxpr/sub | solution.py:101
  102.4 2.7 %fusion.18 = bf16[2,896,64]{1,2,0:T(8,128)(2,1)S(1)} fusion(bf16[2,896,64]{2,1,0:T(8,128)(2,1)} %reshape.297, bf16[2,896,896]{1,2,0:T(8,128)(2,1)} %get-tuple-element.81, f32[2,896]{1,0:T(2,128)S(1)} %get-tuple-element.80), kind=kOutput, calls=%fused_computation.43 | convolution fusion | flops 205750272 | bytes 3677184 | tf_op jit(solution)/shard_map/while/body/eval_jaxpr/gqk,gkd->gqd/dot_general | solution.py:103
  106.0 1.3 reshape_reshape_transpose.3
  108.2 3.5 %all-to-all-start.3 = ((bf16[2,448,128]{2,0,1:T(2,128)(2,1)}), bf16[2,448,128]{2,0,1:T(2,128)(2,1)S(1)}, u32[]{:S(2)}, u32[]{:S(2)}) async-start(bf16[2,448,128]{2,0,1:T(2,128)(2,1)} %copy.44), calls=%async_computation.3 | async-start | bytes 458752 | tf_op jit(solution)/shard_map/all_to_all | solution.py:173
  113.2 8.0 %all-to-all-done.3 = bf16[2,448,128]{2,0,1:T(2,128)(2,1)S(1)} async-done(((bf16[2,448,128]{2,0,1:T(2,128)(2,1)}), bf16[2,448,128]{2,0,1:T(2,128)(2,1)S(1)}, u32[]{:S(2)}, u32[]{:S(2)}) %all-to-all-start.3) | async-done | bytes 229408 | tf_op jit(solution)/shard_map/all_to_all | solution.py:173
  123.9 1.9 %copy.46 = bf16[2,1,56,16,64]{4,3,2,0,1:T(8,128)(2,1)} copy(bf16[2,1,56,16,64]{4,2,3,0,1:T(8,128)(2,1)} %bitcast.91) | data formatting | bytes 458752 | tf_op jit(solution)/shard_map/transpose | solution.py:72
  125.7 1.4 %dot_general.28 = bf16[2,56,1024]{2,1,0:T(8,128)(2,1)S(1)} reshape(bf16[2,1,56,16,64]{4,3,2,0,1:T(8,128)(2,1)} %copy.46) | data formatting | bytes 458752 | tf_op jit(solution)/shard_map/dot_general | solution.py:181
  127.1 1.8 %fusion.80 = (f32[2,56]{1,0:T(2,128)S(1)}, f32[2,56,1536]{2,1,0:T(8,128)S(1)}) fusion(f32[2,56,1536]{2,1,0:T(8,128)} %copy-done.1, bf16[2,56,1024]{2,1,0:T(8,128)(2,1)S(1)} %dot_general.28, bf16[1024,1536]{1,0:T(8,128)(2,1)S(1)} %copy-done, f32[1536]{0:T(1024)S(1)} %copy-done.5), kind=kOutput, calls=%fused_computation.193 | convolution fusion | flops 352837504 | bytes 4757952 | tf_op jit(solution)/shard_map/dot_general | solution.py:181
  (45 shorter events, 12.6 us)
Async XLA Ops:
  0.6 126.5 %copy-start = (bf16[1024,1536]{1,0:T(8,128)(2,1)S(1)}, bf16[1024,1536]{1,0:T(8,128)(2,1)}, u32[]{:S(2)}) copy-start(bf16[1024,1536]{1,0:T(8,128)(2,1)} %param.18) | copy-start | bytes 9437188
  3.4 23.6 %collective-permute-start = (bf16[2,15,1536]{2,1,0:T(8,128)(2,1)}, bf16[2,15,1536]{2,1,0:T(8,128)(2,1)}, u32[]{:S(2)}, u32[]{:S(2)}) collective-permute-start(bf16[2,15,1536]{2,1,0:T(8,128)(2,1)} %get-tuple-element.74), channel_id=1, source_target_pairs={{0,1},{1,2},{2,3},{3,4},{4,5},{5,6},{6,7},{7,8},{8,9},{9,10},{10,1... | collective-permute-start | bytes 276488 | tf_op jit(solution)/shard_map/ppermute | solution.py:22
  6.4 20.5 %collective-permute-start.1 = (bf16[2,15,1536]{2,1,0:T(8,128)(2,1)}, bf16[2,15,1536]{2,1,0:T(8,128)(2,1)}, u32[]{:S(2)}, u32[]{:S(2)}) collective-permute-start(bf16[2,15,1536]{2,1,0:T(8,128)(2,1)} %get-tuple-element.75), channel_id=1, source_target_pairs={{1,0},{2,1},{3,2},{4,3},{5,4},{6,5},{7,6},{8,7},{9,8},{10,9},{11,1... | collective-permute-start | bytes 276488 | tf_op jit(solution)/shard_map/ppermute | solution.py:24
  35.2 7.5 %copy-start.1 = (f32[2,56,1536]{2,1,0:T(8,128)}, f32[2,56,1536]{2,1,0:T(8,128)S(1)}, u32[]{:S(2)}) copy-start(f32[2,56,1536]{2,1,0:T(8,128)S(1)} %get-tuple-element.65) | copy-start | bytes 2064388
  42.7 1.8 %copy-start.2 = (f32[2,56,3,16,64]{4,1,3,2,0:T(8,128)}, f32[2,56,3,16,64]{4,1,3,2,0:T(8,128)S(1)}, u32[]{:S(2)}) copy-start(f32[2,56,3,16,64]{4,1,3,2,0:T(8,128)S(1)} %fusion.60) | copy-start | bytes 4128772
  47.5 18.7 %all-to-all-start.1 = ((bf16[32,28,128]{2,1,0:T(8,128)(2,1)}), bf16[32,28,128]{2,1,0:T(8,128)(2,1)S(1)}, u32[]{:S(2)}, u32[]{:S(2)}) async-start(bf16[32,28,128]{2,1,0:T(8,128)(2,1)} %reshape.294), calls=%async_computation.1 | async-start | bytes 524288 | tf_op jit(solution)/shard_map/all_to_all | solution.py:152
  66.2 14.2 %all-to-all-start = ((bf16[32,28,128]{2,1,0:T(8,128)(2,1)}), bf16[32,28,128]{2,1,0:T(8,128)(2,1)}, u32[]{:S(2)}, u32[]{:S(2)}) async-start(bf16[32,28,128]{2,1,0:T(8,128)(2,1)} %reshape.293), calls=%async_computation | async-start | bytes 524288 | tf_op jit(solution)/shard_map/all_to_all | solution.py:151
  80.4 14.2 %all-to-all-start.2 = ((bf16[32,28,128]{2,1,0:T(8,128)(2,1)}), bf16[32,28,128]{2,1,0:T(8,128)(2,1)}, u32[]{:S(2)}, u32[]{:S(2)}) async-start(bf16[32,28,128]{2,1,0:T(8,128)(2,1)} %reshape.296), calls=%async_computation.2 | async-start | bytes 524288 | tf_op jit(solution)/shard_map/all_to_all | solution.py:153
  102.4 9.4 %copy-start.6 = (f32[56,100]{1,0:T(8,128)S(1)}, f32[56,100]{1,0:T(8,128)}, u32[]{:S(2)}) copy-start(f32[56,100]{1,0:T(8,128)} %param.11) | copy-start | bytes 67204
  102.4 24.8 %copy-start.5 = (f32[1536]{0:T(1024)S(1)}, f32[1536]{0:T(1024)}, u32[]{:S(2)}) copy-start(f32[1536]{0:T(1024)} %get-tuple-element.60) | copy-start | bytes 18436
  108.2 13.0 %all-to-all-start.3 = ((bf16[2,448,128]{2,0,1:T(2,128)(2,1)}), bf16[2,448,128]{2,0,1:T(2,128)(2,1)S(1)}, u32[]{:S(2)}, u32[]{:S(2)}) async-start(bf16[2,448,128]{2,0,1:T(2,128)(2,1)} %copy.44), calls=%async_computation.3 | async-start | bytes 458752 | tf_op jit(solution)/shard_map/all_to_all | solution.py:173
  121.2 0.7 copy-start.3
  127.1 3.0 %copy-start.4 = (bf16[1536,100]{0,1:T(8,128)(2,1)S(1)}, bf16[1536,100]{0,1:T(8,128)(2,1)}, u32[]{:S(2)}) copy-start(bf16[1536,100]{0,1:T(8,128)(2,1)} %param.19) | copy-start | bytes 921604
where the time goes:
time: 134 us; the launch traced here: 132 us
  local copies, waits for them, and re-layouts  43.5 us (32%)
  starting transfers between devices  25.1 us (19%)
  waiting for transfers between devices  24.8 us (19%)
  other arithmetic  17.8 us (13%)
  matrix products  17.7 us (13%)
  between operations  3.05 us (2%)
    unnamed x18, local copies, waits for them, and re-layouts  14.9 us
    all_to_all x1, starting transfers between devices, per_device(): lax.all_to_all(sent[1], 'seq', split_axis=0, concat_axis=1, tiled=True)  8.67 us
    reduce_sum x1, other arithmetic, layer_norm(): mean_value = jnp.mean(values, axis=-1, keepdims=True)  8.24 us
    all_to_all x1, waiting for transfers between devices, per_device(): lax.all_to_all(attended_group.reshape(groups, -1, 2 * HEAD_DIM), 'seq', s...  7.96 us
    dot_general x1, matrix products, per_device(): jnp.dot(normed.reshape(-1, model_width), w_qkv, preferred_element_type=jn...  7.27 us
    all_to_all x1, waiting for transfers between devices, per_device(): lax.all_to_all(sent[0], 'seq', split_axis=0, concat_axis=1, tiled=True)  6.01 us
    reshape x3, local copies, waits for them, and re-layouts, to_groups(): grouped.reshape(copies * HEADS * subs, frame_rows // (2 * subs), 2 * HEAD...  5.91 us
    all_to_all x1, waiting for transfers between devices, per_device(): lax.all_to_all(sent[1], 'seq', split_axis=0, concat_axis=1, tiled=True)  5.86 us
  transfers between devices with their start and end apart: 6, of which 4 were waited for; matrix products, arithmetic and copies ran while one was open for 25% of the time, Pallas kernels for 0%

commit v1 on v0

--- a/solution.py
+++ b/solution.py
@@ -2,6 +2,7 @@
 import jax.numpy as jnp
 from jax import lax
 from jax.sharding import PartitionSpec as P
+from jax.lax import all_to_all, axis_size
 
 HEADS = 16
 HEAD_DIM = 64
@@ -115,6 +116,15 @@
 def per_device(
     hidden, latent, lengths, step_index, guidance, modulation, conv_kernel, w_qkv, w_out, w_mel
 ):
+
+    def define_joints(page, ndim_at, in_dim):
+        spare = axis_size("seq")
+        earlier = jnp.split(page, spare, axis=ndim_at)
+        long_array = jnp.stack(earlier)
+        heard = all_to_all(long_array, "seq", 0, 0)
+        later = jnp.concatenate(heard, axis=in_dim)
+        return later
+
     copies, frame_rows, model_width = hidden.shape
     offset = lax.axis_index("seq") * frame_rows
     positions = offset + jnp.arange(frame_rows, dtype=jnp.int32)
@@ -170,13 +180,7 @@
     key_flat = key_group.reshape(groups, -1, HEAD_DIM)
     value_flat = value_group.reshape(groups, -1, HEAD_DIM)
     attended_group = attend_local(query_flat, key_flat, value_flat, key_rows < length)
-    returned = lax.all_to_all(
-        attended_group.reshape(groups, -1, 2 * HEAD_DIM),
-        "seq",
-        split_axis=1,
-        concat_axis=0,
-        tiled=True,
-    )
+    returned = define_joints(attended_group.reshape(groups, -1, 2 * HEAD_DIM), 1, in_dim=0)
     attended = from_groups(returned, copies, frame_rows, subs)
     branch = jnp.dot(
         attended.reshape(copies * frame_rows, -1), w_out, preferred_element_type=jnp.float32

time: 134 us -> 134 us (level)
    another operation x0 -> x3, local copies, waits for them, and re-layouts: none -> 1.89 us  [the longest x1 1.01 us: from_groups(): grouped.reshape(copies, HEADS, subs, frame_rows // subs, HEAD_DIM)]
    unnamed x18 -> x31, local copies, waits for them, and re-layouts: 14.9 us -> 14.4 us
where the time goes in v1:
time: 134 us; the launch traced here: 132 us
  local copies, waits for them, and re-layouts  43 us (32%)
  starting transfers between devices  25.7 us (19%)
  waiting for transfers between devices  24.8 us (19%)
  other arithmetic  17.8 us (13%)
  matrix products  17.7 us (13%)
  between operations  3.12 us (2%)
    unnamed x31, local copies, waits for them, and re-layouts  14.4 us
    all_to_all x1, starting transfers between devices, per_device(): lax.all_to_all(sent[1], 'seq', split_axis=0, concat_axis=1, tiled=True)  8.67 us
    reduce_sum x1, other arithmetic, layer_norm(): mean_value = jnp.mean(values, axis=-1, keepdims=True)  8.24 us
    all_to_all x1, waiting for transfers between devices, define_joints(): heard = all_to_all(long_array, 'seq', 0, 0)  8.01 us
    dot_general x1, matrix products, per_device(): jnp.dot(normed.reshape(-1, model_width), w_qkv, preferred_element_type=jn...  7.27 us
    all_to_all x1, waiting for transfers between devices, per_device(): lax.all_to_all(sent[0], 'seq', split_axis=0, concat_axis=1, tiled=True)  6.01 us
    reshape x3, local copies, waits for them, and re-layouts, to_groups(): grouped.reshape(copies * HEADS * subs, frame_rows // (2 * subs), 2 * HEAD...  5.91 us
    all_to_all x1, waiting for transfers between devices, per_device(): lax.all_to_all(sent[1], 'seq', split_axis=0, concat_axis=1, tiled=True)  5.86 us
  transfers between devices with their start and end apart: 6, of which 4 were waited for; matrix products, arithmetic and copies ran while one was open for 25% of the time, Pallas kernels for 0%

profile of v1, /device:TPU:0, one launch (start us, length us, event | category | flops | bytes accessed | tf_op | source)
XLA Modules:
  0.0 132.1 jit_solution(2915310834250251281)
XLA Ops:
  1.5 1.2 broadcast_multiply_fusion
  3.4 3.0 %collective-permute-start = (bf16[2,15,1536]{2,1,0:T(8,128)(2,1)}, bf16[2,15,1536]{2,1,0:T(8,128)(2,1)}, u32[]{:S(2)}, u32[]{:S(2)}) collective-permute-start(bf16[2,15,1536]{2,1,0:T(8,128)(2,1)} %get-tuple-element.74), channel_id=1, source_target_pairs={{0,1},{1,2},{2,3},{3,4},{4,5},{5,6},{6,7},{7,8},{8,9},{9,10},{10,1... | collective-permute-start | bytes 276488 | tf_op jit(solution)/shard_map/ppermute | solution.py:23
  6.4 1.3 collective-permute-start.1
  7.7 2.5 %slice_reduce_fusion.33 = (f32[1536]{0:T(1024)S(1)}, f32[1536]{0:T(1024)S(1)}, f32[1536]{0:T(1024)S(1)}, f32[1536]{0:T(1024)S(1)}, f32[1536]{0:T(1024)S(1)}, /*i...) fusion(f32[31,1536]{1,0:T(8,128)} %param.16), kind=kLoop, calls=%fused_computation.209 | loop fusion | bytes 233472 | tf_op jit(solution)/shard_map/slice | solution.py:138
  10.2 2.1 %slice_reduce_fusion.32 = (f32[1536]{0:T(1024)}, f32[1536]{0:T(1024)}, f32[1536]{0:T(1024)}, f32[1536]{0:T(1024)}, f32[1536]{0:T(1024)}, /*index=5*/f32[1536]{0:...) fusion(f32[31,1536]{1,0:T(8,128)} %param.16), kind=kLoop, calls=%fused_computation.208 | loop fusion | bytes 147456 | tf_op jit(solution)/shard_map/slice | solution.py:138
  12.3 12.7 %copy.32 = bf16[1536,3072]{0,1:T(8,128)(2,1)} copy(bf16[1536,3072]{1,0:T(8,128)(2,1)} %param.17) | data formatting | bytes 18874368 | tf_op args[7]
  25.2 1.7 %add_reduce_fusion = (f32[1536]{0:T(1024)S(1)}, f32[1536]{0:T(1024)S(1)}, f32[1536]{0:T(1024)S(1)}, f32[1536]{0:T(1024)}, f32[1536]{0:T(1024)}) fusion(f32[5,1536]{1,0:T(8,128)} %param.15), kind=kLoop, calls=%fused_computation.175 | loop fusion | flops 3072 | bytes 61440 | tf_op jit(solution)/shard_map/add | solution.py:40
  26.9 8.2 %fusion.74 = (f32[2,56]{1,0:T(2,128)S(1)}, f32[2,56,1536]{2,1,0:T(8,128)S(1)}) fusion(bf16[2,15,1536]{2,1,0:T(8,128)(2,1)} %collective-permute-done.1, bf16[2,56,1536]{2,1,0:T(8,128)(2,1)S(1)} %broadcast_multiply_fusion, f32[1536]{0:T(1024)} %get-tuple-element.55, f32[1536]{0:T(1024)} %get-tuple-element.56, f32[1536]{0:T(1024)S(1)} %get-tuple-element.27, ...), kind=kLoop, calls=%fused_computation.221 | loop fusion | flops 33030032 | bytes 1751488 | tf_op jit(solution)/shard_map/reduce_sum | solution.py:37
  35.4 7.3 %fusion.60 = f32[2,56,3,16,64]{4,1,3,2,0:T(8,128)S(1)} fusion(bf16[3,16,64,1536,1]{3,2,1,0,4:T(8,128)(2,1)} %bitcast.151, f32[2,56,1536]{2,1,0:T(8,128)S(1)} %get-tuple-element.65, f32[1536]{0:T(1024)S(1)} %get-tuple-element.58, f32[1536]{0:T(1024)S(1)} %get-tuple-element.59, f32[2,56]{1,0:T(2,128)S(1)} %add_rsqrt_fusion.1, ...), kind=kOutput, calls=%fused_computation.123 | convolution fusion | flops 1057824768 | bytes 11514752 | tf_op jit(solution)/shard_map/dot_general | solution.py:143
  42.9 1.7 %fusion.28 = (bf16[2,1,56,16,32]{4,2,3,0,1:T(8,128)(2,1)S(1)}, bf16[2,1,56,16,32]{4,2,3,0,1:T(8,128)(2,1)S(1)}, bf16[2,1,56,16,32]{4,2,3,0,1:T(8,128)(2,1)}, bf16[2,1,56,16,32]{4,2,3,0,1:T(8,128)(2,1)}) fusion(f32[2,56,16,64]{3,1,2,0:T(8,128)S(1)} %get-tuple-element.68, f32[56,32]{1,0:T(8,128)S(1)} %get-tuple-element.79, f32[56,32]{1,0:T(8,128)S(1)} %get-tuple-element.78, ...), kind=kLoop, calls=%fused_computation.61 | loop fusion | flops 917504 | bytes 1390592 | tf_op jit(solution)/shard_map/concatenate | solution.py:55
  44.5 1.0 maximum_bitcast_fusion.1
  45.6 2.0 %reshape.290 = bf16[32,28,128]{2,1,0:T(8,128)(2,1)} reshape(bf16[2,16,1,56,64]{4,3,1,0,2:T(8,128)(2,1)} %maximum_bitcast_fusion.1) | data formatting | bytes 458752 | tf_op jit(solution)/shard_map/reshape | solution.py:69
  47.5 8.7 %all-to-all-start.1 = ((bf16[32,28,128]{2,1,0:T(8,128)(2,1)}), bf16[32,28,128]{2,1,0:T(8,128)(2,1)S(1)}, u32[]{:S(2)}, u32[]{:S(2)}) async-start(bf16[32,28,128]{2,1,0:T(8,128)(2,1)} %reshape.290), calls=%async_computation.1 | async-start | bytes 524288 | tf_op jit(solution)/shard_map/all_to_all | solution.py:162
  56.2 2.2 %maximum_bitcast_fusion = bf16[2,16,1,56,64]{4,3,1,0,2:T(8,128)(2,1)} fusion(bf16[2,1,56,16,32]{4,2,3,0,1:T(8,128)(2,1)} %get-tuple-element.76, bf16[2,1,56,16,32]{4,2,3,0,1:T(8,128)(2,1)} %get-tuple-element.77), kind=kLoop, calls=%fused_computation.64 | loop fusion | flops 458752 | bytes 458752 | tf_op jit(solution)/shard_map/transpose | solution.py:66
  58.4 2.0 %reshape.289 = bf16[32,28,128]{2,1,0:T(8,128)(2,1)} reshape(bf16[2,16,1,56,64]{4,3,1,0,2:T(8,128)(2,1)} %maximum_bitcast_fusion) | data formatting | bytes 458752 | tf_op jit(solution)/shard_map/reshape | solution.py:69
  60.4 5.9 %all-to-all-done.1 = bf16[32,28,128]{2,1,0:T(8,128)(2,1)S(1)} async-done(((bf16[32,28,128]{2,1,0:T(8,128)(2,1)}), bf16[32,28,128]{2,1,0:T(8,128)(2,1)S(1)}, u32[]{:S(2)}, u32[]{:S(2)}) %all-to-all-start.1) | async-done | bytes 229408 | tf_op jit(solution)/shard_map/all_to_all | solution.py:162
  66.2 4.2 %all-to-all-start = ((bf16[32,28,128]{2,1,0:T(8,128)(2,1)}), bf16[32,28,128]{2,1,0:T(8,128)(2,1)}, u32[]{:S(2)}, u32[]{:S(2)}) async-start(bf16[32,28,128]{2,1,0:T(8,128)(2,1)} %reshape.289), calls=%async_computation | async-start | bytes 524288 | tf_op jit(solution)/shard_map/all_to_all | solution.py:161
  70.4 2.0 %fusion.30 = bf16[2,16,1,56,64]{4,3,1,0,2:T(8,128)(2,1)} fusion(f32[2,56,3,16,64]{4,1,3,2,0:T(8,128)} %copy-done.2), kind=kLoop, calls=%fused_computation.63 | loop fusion | bytes 458752 | tf_op jit(solution)/shard_map/transpose | solution.py:66
  72.5 2.0 %reshape.292 = bf16[32,28,128]{2,1,0:T(8,128)(2,1)} reshape(bf16[2,16,1,56,64]{4,3,1,0,2:T(8,128)(2,1)} %fusion.30) | data formatting | bytes 458752 | tf_op jit(solution)/shard_map/reshape | solution.py:69
  74.4 6.0 %all-to-all-done = bf16[32,28,128]{2,1,0:T(8,128)(2,1)} async-done(((bf16[32,28,128]{2,1,0:T(8,128)(2,1)}), bf16[32,28,128]{2,1,0:T(8,128)(2,1)}, u32[]{:S(2)}, u32[]{:S(2)}) %all-to-all-start) | async-done | bytes 229408 | tf_op jit(solution)/shard_map/all_to_all | solution.py:161
  80.4 4.4 %all-to-all-start.2 = ((bf16[32,28,128]{2,1,0:T(8,128)(2,1)}), bf16[32,28,128]{2,1,0:T(8,128)(2,1)}, u32[]{:S(2)}, u32[]{:S(2)}) async-start(bf16[32,28,128]{2,1,0:T(8,128)(2,1)} %reshape.292), calls=%async_computation.2 | async-start | bytes 524288 | tf_op jit(solution)/shard_map/all_to_all | solution.py:163
  85.7 2.0 %reshape.291 = bf16[2,896,64]{2,1,0:T(8,128)(2,1)} reshape(bf16[2,16,28,128]{3,2,1,0:T(8,128)(2,1)} %bitcast.155) | data formatting | bytes 458752 | tf_op jit(solution)/shard_map/reshape | solution.py:180
  88.7 1.0 squeeze.26
  89.7 4.9 %all-to-all-done.2 = bf16[32,28,128]{2,1,0:T(8,128)(2,1)} async-done(((bf16[32,28,128]{2,1,0:T(8,128)(2,1)}), bf16[32,28,128]{2,1,0:T(8,128)(2,1)}, u32[]{:S(2)}, u32[]{:S(2)}) %all-to-all-start.2) | async-done | bytes 229408 | tf_op jit(solution)/shard_map/all_to_all | solution.py:163
  96.6 5.7 %fusion.79 = (f32[2,896]{1,0:T(2,128)S(1)}, bf16[2,896,896]{1,2,0:T(8,128)(2,1)}) fusion(pred[896]{0:T(1024)(128)(4,1)S(1)} %lt.36, bf16[2,896,64]{2,1,0:T(8,128)(2,1)} %squeeze.26, bf16[2,896,64]{2,1,0:T(8,128)(2,1)} %reshape.291), kind=kOutput, calls=%fused_computation.224 | convolution fusion | flops 215155584 | bytes 3678080 | tf_op jit(solution)/shard_map/while/body/eval_jaxpr/sub | solution.py:102
  102.4 2.7 %fusion.18 = bf16[2,896,64]{1,2,0:T(8,128)(2,1)S(1)} fusion(bf16[2,896,64]{2,1,0:T(8,128)(2,1)} %reshape.293, bf16[2,896,896]{1,2,0:T(8,128)(2,1)} %get-tuple-element.81, f32[2,896]{1,0:T(2,128)S(1)} %get-tuple-element.80), kind=kOutput, calls=%fused_computation.43 | convolution fusion | flops 205750272 | bytes 3677184 | tf_op jit(solution)/shard_map/while/body/eval_jaxpr/gqk,gkd->gqd/dot_general | solution.py:104
  106.0 1.3 reshape_reshape_transpose.3
  108.4 4.2 %all-to-all-start.3 = ((bf16[16,2,28,128]{3,1,2,0:T(2,128)(2,1)}), bf16[16,2,28,128]{3,1,2,0:T(2,128)(2,1)}, u32[]{:S(2)}, u32[]{:S(2)}) async-start(bf16[16,2,28,128]{3,1,2,0:T(2,128)(2,1)} %copy.42), calls=%async_computation.3 | async-start | bytes 458752 | tf_op jit(solution)/shard_map/all_to_all | solution.py:124
  114.1 8.0 %all-to-all-done.3 = bf16[16,2,28,128]{3,1,2,0:T(2,128)(2,1)} async-done(((bf16[16,2,28,128]{3,1,2,0:T(2,128)(2,1)}), bf16[16,2,28,128]{3,1,2,0:T(2,128)(2,1)}, u32[]{:S(2)}, u32[]{:S(2)}) %all-to-all-start.3) | async-done | bytes 229408 | tf_op jit(solution)/shard_map/all_to_all | solution.py:124
  124.1 1.9 %copy.44 = bf16[2,1,56,16,64]{4,3,2,0,1:T(8,128)(2,1)} copy(bf16[2,1,56,16,64]{4,2,3,0,1:T(8,128)(2,1)} %bitcast.152) | data formatting | bytes 458752 | tf_op jit(solution)/shard_map/transpose | solution.py:73
  126.0 1.4 %dot_general.28 = bf16[2,56,1024]{2,1,0:T(8,128)(2,1)S(1)} reshape(bf16[2,1,56,16,64]{4,3,2,0,1:T(8,128)(2,1)} %copy.44) | data formatting | bytes 458752 | tf_op jit(solution)/shard_map/dot_general | solution.py:185
  127.4 1.8 %fusion.80 = (f32[2,56]{1,0:T(2,128)S(1)}, f32[2,56,1536]{2,1,0:T(8,128)S(1)}) fusion(f32[2,56,1536]{2,1,0:T(8,128)} %copy-done.1, bf16[2,56,1024]{2,1,0:T(8,128)(2,1)S(1)} %dot_general.28, bf16[1024,1536]{1,0:T(8,128)(2,1)S(1)} %copy-done, f32[1536]{0:T(1024)S(1)} %copy-done.4), kind=kOutput, calls=%fused_computation.225 | convolution fusion | flops 352837504 | bytes 4757952 | tf_op jit(solution)/shard_map/dot_general | solution.py:185
  (59 shorter events, 12.1 us)
Async XLA Ops:
  0.6 126.7 %copy-start = (bf16[1024,1536]{1,0:T(8,128)(2,1)S(1)}, bf16[1024,1536]{1,0:T(8,128)(2,1)}, u32[]{:S(2)}) copy-start(bf16[1024,1536]{1,0:T(8,128)(2,1)} %param.18) | copy-start | bytes 9437188
  3.4 23.6 %collective-permute-start = (bf16[2,15,1536]{2,1,0:T(8,128)(2,1)}, bf16[2,15,1536]{2,1,0:T(8,128)(2,1)}, u32[]{:S(2)}, u32[]{:S(2)}) collective-permute-start(bf16[2,15,1536]{2,1,0:T(8,128)(2,1)} %get-tuple-element.74), channel_id=1, source_target_pairs={{0,1},{1,2},{2,3},{3,4},{4,5},{5,6},{6,7},{7,8},{8,9},{9,10},{10,1... | collective-permute-start | bytes 276488 | tf_op jit(solution)/shard_map/ppermute | solution.py:23
  6.4 20.5 %collective-permute-start.1 = (bf16[2,15,1536]{2,1,0:T(8,128)(2,1)}, bf16[2,15,1536]{2,1,0:T(8,128)(2,1)}, u32[]{:S(2)}, u32[]{:S(2)}) collective-permute-start(bf16[2,15,1536]{2,1,0:T(8,128)(2,1)} %get-tuple-element.75), channel_id=1, source_target_pairs={{1,0},{2,1},{3,2},{4,3},{5,4},{6,5},{7,6},{8,7},{9,8},{10,9},{11,1... | collective-permute-start | bytes 276488 | tf_op jit(solution)/shard_map/ppermute | solution.py:25
  35.2 7.5 %copy-start.1 = (f32[2,56,1536]{2,1,0:T(8,128)}, f32[2,56,1536]{2,1,0:T(8,128)S(1)}, u32[]{:S(2)}) copy-start(f32[2,56,1536]{2,1,0:T(8,128)S(1)} %get-tuple-element.65) | copy-start | bytes 2064388
  42.7 1.8 %copy-start.2 = (f32[2,56,3,16,64]{4,1,3,2,0:T(8,128)}, f32[2,56,3,16,64]{4,1,3,2,0:T(8,128)S(1)}, u32[]{:S(2)}) copy-start(f32[2,56,3,16,64]{4,1,3,2,0:T(8,128)S(1)} %fusion.60) | copy-start | bytes 4128772
  47.5 18.7 %all-to-all-start.1 = ((bf16[32,28,128]{2,1,0:T(8,128)(2,1)}), bf16[32,28,128]{2,1,0:T(8,128)(2,1)S(1)}, u32[]{:S(2)}, u32[]{:S(2)}) async-start(bf16[32,28,128]{2,1,0:T(8,128)(2,1)} %reshape.290), calls=%async_computation.1 | async-start | bytes 524288 | tf_op jit(solution)/shard_map/all_to_all | solution.py:162
  66.2 14.2 %all-to-all-start = ((bf16[32,28,128]{2,1,0:T(8,128)(2,1)}), bf16[32,28,128]{2,1,0:T(8,128)(2,1)}, u32[]{:S(2)}, u32[]{:S(2)}) async-start(bf16[32,28,128]{2,1,0:T(8,128)(2,1)} %reshape.289), calls=%async_computation | async-start | bytes 524288 | tf_op jit(solution)/shard_map/all_to_all | solution.py:161
  80.4 14.2 %all-to-all-start.2 = ((bf16[32,28,128]{2,1,0:T(8,128)(2,1)}), bf16[32,28,128]{2,1,0:T(8,128)(2,1)}, u32[]{:S(2)}, u32[]{:S(2)}) async-start(bf16[32,28,128]{2,1,0:T(8,128)(2,1)} %reshape.292), calls=%async_computation.2 | async-start | bytes 524288 | tf_op jit(solution)/shard_map/all_to_all | solution.py:163
  102.4 10.2 %copy-start.5 = (f32[56,100]{1,0:T(8,128)S(1)}, f32[56,100]{1,0:T(8,128)}, u32[]{:S(2)}) copy-start(f32[56,100]{1,0:T(8,128)} %param.11) | copy-start | bytes 67204
  102.4 25.0 %copy-start.4 = (f32[1536]{0:T(1024)S(1)}, f32[1536]{0:T(1024)}, u32[]{:S(2)}) copy-start(f32[1536]{0:T(1024)} %get-tuple-element.60) | copy-start | bytes 18436
  108.4 13.7 %all-to-all-start.3 = ((bf16[16,2,28,128]{3,1,2,0:T(2,128)(2,1)}), bf16[16,2,28,128]{3,1,2,0:T(2,128)(2,1)}, u32[]{:S(2)}, u32[]{:S(2)}) async-start(bf16[16,2,28,128]{3,1,2,0:T(2,128)(2,1)} %copy.42), calls=%async_computation.3 | async-start | bytes 458752 | tf_op jit(solution)/shard_map/all_to_all | solution.py:124
  127.3 3.0 %copy-start.3 = (bf16[1536,100]{0,1:T(8,128)(2,1)S(1)}, bf16[1536,100]{0,1:T(8,128)(2,1)}, u32[]{:S(2)}) copy-start(bf16[1536,100]{0,1:T(8,128)(2,1)} %param.19) | copy-start | bytes 921604
